TPU v7x, 512 devices: a whole 4x4x16 slice. The times are simulated.
512 devices in a mesh: expert: 64 (over x, z), dp: 4 (over y), test: 2 (over core).
Axes of the slice: x: 4, y: 4, z: 16, core: 2. Of those that a mesh axis runs over, the one named last changes fastest.
Arguments:
- tokens: bfloat16 [16384, 3584], P(('expert', 'dp'), 'test'), may hold values from -6 to 6
- out_grad: bfloat16 [16384, 3584], P(('expert', 'dp'), 'test'), may hold values from -6 to 6
- route_ids: int32 [16384, 8], P(('expert', 'dp')), may hold values from 0 to 255, as said below
- route_slots: int32 [16384, 8], P(('expert', 'dp')), may hold values from -1 to 1, as said below
- route_weight: bfloat16 [16384, 8], P(('expert', 'dp')), may hold values from 0.19921875 to 1
- w_gate: bfloat16 [64, 3584, 1024], P('expert', None, ('dp', 'test')), may hold values from -0.09375 to 0.09375
- w_up: bfloat16 [64, 3584, 1024], P('expert', None, ('dp', 'test')), may hold values from -0.09375 to 0.09375
- w_down: bfloat16 [64, 1024, 3584], P('expert', ('dp', 'test')), may hold values from -0.1875 to 0.1875
- proj_hidden: bfloat16 [64, 64, 1024], P('expert', None, ('dp', 'test')), may hold values from -0.1875 to 0.1875
- proj_grad: bfloat16 [64, 64, 3584], P('expert'), may hold values from -0.09375 to 0.09375
- test_feats: bfloat16 [64, 256, 4096], P('expert', 'test'), may hold values from -0.09375 to 0.09375
Outputs:
- in_grad: bfloat16 [16384, 3584], P(('expert', 'dp'), 'test')
- scores: float32 [16384, 256], P(('expert', 'dp'), 'test')
Inputs may be any that keep to these rules, and one draw needn't show every extreme that they name: `route_ids`: each row names 8 different experts. `route_slots`: A route's slot is -1 exactly when its expert is 64 or more, or when 2 earlier tokens of the same aligned block of 64 rows already take that expert; otherwise it is the number of earlier tokens of that block routed to that expert.
All inputs are finite; a program needn't handle non-finite values.
Results may differ from a plain program's by a relative error of at most 0.0065.
Values may be sent and summed in bfloat16 or wider, within the bound.
A program may use at most 64 MiB of HBM per device.

v0:
```python
import jax
import jax.numpy as jnp
from jax import lax
from jax.sharding import PartitionSpec as P

CAP = 2


def pick_tables(ids_in, slots_in, weights_in, experts):
    live_mask = (slots_in >= 0) & (ids_in < experts)
    slot_code = jnp.where(live_mask, ids_in * CAP + slots_in, -1)
    columns = jnp.arange(experts * CAP, dtype=jnp.int32)
    matches = slot_code[:, :, None] == columns[None, None, :]
    picks = jnp.sum(matches.astype(jnp.float32), axis=1)
    weighted = jnp.sum(jnp.where(matches, weights_in.astype(jnp.float32)[:, :, None], 0.0), axis=1)
    return (picks, weighted)


def expert_pass(flat_in, flat_grad, gate_w, up_w, down_w, hid_proj):
    gate_pre = jnp.dot(flat_in, gate_w, preferred_element_type=jnp.float32)
    up_pre = jnp.dot(flat_in, up_w, preferred_element_type=jnp.float32)
    sigmoid_gate = jax.nn.sigmoid(gate_pre)
    act_gate = gate_pre * sigmoid_gate
    hidden = (act_gate * up_pre).astype(jnp.bfloat16)
    proj_part = lax.dot_general(
        hidden, hid_proj, (((1,), (1,)), ((), ())), preferred_element_type=jnp.float32
    )
    hid_grad = lax.dot_general(
        flat_grad, down_w, (((1,), (1,)), ((), ())), preferred_element_type=jnp.float32
    )
    up_grad = (hid_grad * act_gate).astype(jnp.bfloat16)
    gate_grad = (hid_grad * up_pre * sigmoid_gate * (1.0 + gate_pre * (1.0 - sigmoid_gate))).astype(
        jnp.bfloat16
    )
    return (proj_part, gate_grad, up_grad)


def score_rows(hidden_vec, grad_vec, test_rows):
    row_total = hidden_vec.shape[0]
    feature = (
        (hidden_vec[:, :, None] * grad_vec[:, None, :]).reshape(row_total, -1).astype(jnp.bfloat16)
    )
    return lax.dot_general(
        feature, test_rows, (((1,), (1,)), ((), ())), preferred_element_type=jnp.float32
    )


def on_device(
    tokens,
    out_grad,
    route_ids,
    route_slots,
    route_weight,
    w_gate,
    w_up,
    w_down,
    proj_hidden,
    proj_grad,
    test_feats,
):
    experts = lax.axis_size("expert")
    groups = lax.axis_size("dp")
    halves = lax.axis_size("test")
    tok_rows = tokens.shape[0]
    half_width = tokens.shape[1]
    slots_all = experts * CAP
    full_in, full_grad = (
        lax.all_gather(tokens, "test", axis=1, tiled=True),
        lax.all_gather(out_grad, "test", axis=1, tiled=True),
    )
    full_width = full_in.shape[1]
    grad_proj = proj_grad[0]
    test_rows = test_feats[0]
    own_pick, own_weight = pick_tables(route_ids, route_slots, route_weight, experts)
    all_in, all_grad, all_ids, all_slots, all_weight = (
        lax.all_gather(full_in, "dp", axis=0, tiled=True),
        lax.all_gather(full_grad, "dp", axis=0, tiled=True),
        lax.all_gather(route_ids, "dp", axis=0, tiled=True),
        lax.all_gather(route_slots, "dp", axis=0, tiled=True),
        lax.all_gather(route_weight, "dp", axis=0, tiled=True),
    )
    group_tok = all_in.shape[0]
    pick_all, weight_all = pick_tables(all_ids, all_slots, all_weight, experts)
    owner_idx = jnp.arange(group_tok, dtype=jnp.int32) // tok_rows
    in_group = (owner_idx[None, :] == jnp.arange(groups, dtype=jnp.int32)[:, None]).astype(
        jnp.float32
    )
    select = (
        (pick_all.T.reshape(experts, 1, CAP, group_tok) * in_group.reshape(1, groups, 1, group_tok))
        .reshape(-1, group_tok)
        .astype(jnp.bfloat16)
    )
    select_w = (
        (
            weight_all.T.reshape(experts, 1, CAP, group_tok)
            * in_group.reshape(1, groups, 1, group_tok)
        )
        .reshape(-1, group_tok)
        .astype(jnp.bfloat16)
    )
    in_buf = jnp.dot(select, all_in, preferred_element_type=jnp.float32).astype(jnp.bfloat16)
    grad_buf = jnp.dot(select_w, all_grad, preferred_element_type=jnp.float32).astype(jnp.bfloat16)
    rows_per = groups * CAP
    recv_in, recv_grad = (
        lax.all_to_all(
            in_buf.reshape(experts, rows_per, full_width),
            "expert",
            split_axis=0,
            concat_axis=0,
            tiled=True,
        ),
        lax.all_to_all(
            grad_buf.reshape(experts, rows_per, full_width),
            "expert",
            split_axis=0,
            concat_axis=0,
            tiled=True,
        ),
    )
    flat_in = recv_in.reshape(-1, full_width)
    flat_grad = recv_grad.reshape(-1, full_width)
    gate_w = w_gate[0]
    up_w = w_up[0]
    proj_part, gate_grad, up_grad = expert_pass(
        flat_in, flat_grad, gate_w, up_w, w_down[0], proj_hidden[0]
    )
    parts = lax.dot_general(
        gate_grad, gate_w, (((1,), (1,)), ((), ())), preferred_element_type=jnp.float32
    )
    parts = (
        parts
        + lax.dot_general(
            up_grad, up_w, (((1,), (1,)), ((), ())), preferred_element_type=jnp.float32
        )
    ).astype(jnp.bfloat16)
    hidden_vec = lax.psum(proj_part, ("dp", "test"))
    my_group = lax.axis_index("dp")
    hid_mine = lax.dynamic_index_in_dim(
        hidden_vec.reshape(experts, groups, CAP, -1), my_group, 1, keepdims=False
    ).reshape(slots_all, -1)
    grad_rows = lax.dynamic_index_in_dim(
        recv_grad.reshape(experts, groups, CAP, full_width), my_group, 1, keepdims=False
    ).reshape(slots_all, full_width)
    grad_mine = lax.dot_general(
        grad_rows, grad_proj, (((1,), (1,)), ((), ())), preferred_element_type=jnp.float32
    )
    route_score = (
        score_rows(hid_mine, grad_mine, test_rows).astype(jnp.bfloat16).reshape(experts, CAP, -1)
    )
    back_parts, back_score = (
        lax.all_to_all(
            parts.reshape(experts, rows_per, full_width),
            "expert",
            split_axis=0,
            concat_axis=0,
            tiled=True,
        ),
        lax.all_to_all(route_score, "expert", split_axis=0, concat_axis=0, tiled=True),
    )
    part_rows = back_parts.reshape(-1, full_width)
    first_row = jnp.int32(0)
    pieces = []
    for block_step in range(tok_rows * lax.axis_size(("dp", "test")) // tok_rows):
        block_idx = first_row // tok_rows + block_step
        owner_block = block_idx // halves
        half_idx = block_idx % halves
        picked_cols = lax.dynamic_slice_in_dim(select, owner_block * tok_rows, tok_rows, 1)
        part_cols = lax.dynamic_slice_in_dim(part_rows, half_idx * half_width, half_width, 1)
        pieces.append(
            lax.dot_general(
                picked_cols, part_cols, (((0,), (0,)), ((), ())), preferred_element_type=jnp.float32
            )
        )
    in_grad = lax.psum_scatter(
        jnp.concatenate(pieces, axis=0), ("dp", "test"), scatter_dimension=0, tiled=True
    ).astype(jnp.bfloat16)
    scores_out = jnp.dot(
        own_pick.astype(jnp.bfloat16),
        back_score.reshape(slots_all, -1),
        preferred_element_type=jnp.float32,
    )
    return (in_grad, scores_out)


def solution(mesh):
    placed = (
        P(("expert", "dp"), "test"),
        P(("expert", "dp"), "test"),
        P(("expert", "dp"), None),
        P(("expert", "dp"), None),
        P(("expert", "dp"), None),
        P("expert", None, ("dp", "test")),
        P("expert", None, ("dp", "test")),
        P("expert", ("dp", "test"), None),
        P("expert", None, ("dp", "test")),
        P("expert", None, None),
        P("expert", "test", None),
    )
    return jax.shard_map(
        on_device,
        mesh=mesh,
        in_specs=placed,
        out_specs=(P(("expert", "dp"), "test"), P(("expert", "dp"), "test")),
        check_vma=False,
    )
```

profile of v0, /device:TPU:4, one launch (start us, length us, event | category | flops | bytes accessed | tf_op | source)
XLA Modules:
  0.0 659.0 jit_solution(9366702021190305749)
XLA Ops:
  7.2 3.9 all_gather.26
  11.1 12.7 %all-gather = s32[4,64,8]{1,2,0:T(8,128)S(1)} all-gather(s32[1,64,8]{1,2,0:T(8,128)} %bitcast.65), channel_id=1, replica_groups=mesh['expert'=64,'dp'=4,'test'=2] {'dp'}, dimensions={0}, use_global_device_ids=true | all-gather | bytes 10240 | tf_op jit(solution)/shard_map/all_gather | solution.py:79
  23.8 12.1 %all-gather.1 = s32[4,64,8]{1,2,0:T(8,128)S(1)} all-gather(s32[1,64,8]{1,2,0:T(8,128)} %bitcast.66), channel_id=1, replica_groups=mesh['expert'=64,'dp'=4,'test'=2] {'dp'}, dimensions={0}, use_global_device_ids=true | all-gather | bytes 10240 | tf_op jit(solution)/shard_map/all_gather | solution.py:78
  36.1 10.8 %all-gather.2 = bf16[4,64,8]{1,2,0:T(8,128)(2,1)S(1)} all-gather(bf16[1,64,8]{1,2,0:T(8,128)(2,1)} %bitcast.67), channel_id=1, replica_groups=mesh['expert'=64,'dp'=4,'test'=2] {'dp'}, dimensions={0}, use_global_device_ids=true | all-gather | bytes 5120 | tf_op jit(solution)/shard_map/all_gather | solution.py:80
  49.4 2.8 all-gather.8.cloned.1.call-done
  52.2 4.4 fusion.1
  56.6 16.3 %all-to-all-start.1 = ((bf16[64,8,3584]{2,1,0:T(8,128)(2,1)}), bf16[64,8,3584]{2,1,0:T(8,128)(2,1)}, u32[]{:S(2)}, u32[]{:S(2)}) async-start(bf16[64,8,3584]{2,1,0:T(8,128)(2,1)} %fusion.1), calls=%async_computation.1 | async-start | bytes 7340032 | tf_op jit(solution)/shard_map/all_to_all | solution.py:105
  73.0 2.3 all_gather.24
  75.4 37.0 %all-gather.6.cloned.1.call-done = bf16[256,3584]{1,0:T(8,128)(2,1)} async-done(((bf16[64,3584]{1,0:T(8,128)(2,1)}), bf16[256,3584]{1,0:T(8,128)(2,1)}) %all-gather.6.cloned.1.call-update) | async-done | bytes 1835024 | tf_op jit(solution)/shard_map/all_gather | solution.py:77
  112.4 4.5 fusion
  116.9 118.8 %all-to-all-done.1 = bf16[64,8,3584]{2,1,0:T(8,128)(2,1)} async-done(((bf16[64,8,3584]{2,1,0:T(8,128)(2,1)}), bf16[64,8,3584]{2,1,0:T(8,128)(2,1)}, u32[]{:S(2)}, u32[]{:S(2)}) %all-to-all-start.1) | async-done | bytes 3670048 | tf_op jit(solution)/shard_map/all_to_all | solution.py:105
  235.7 10.0 %all-to-all-start = ((bf16[64,8,3584]{2,1,0:T(8,128)(2,1)}), bf16[64,8,3584]{2,1,0:T(8,128)(2,1)}, u32[]{:S(2)}, u32[]{:S(2)}) async-start(bf16[64,8,3584]{2,1,0:T(8,128)(2,1)} %fusion), calls=%async_computation | async-start | bytes 7340032 | tf_op jit(solution)/shard_map/all_to_all | solution.py:112
  245.7 3.2 fusion.3
  249.0 3.8 fusion.5
  252.8 155.7 %all-to-all-done = bf16[64,8,3584]{2,1,0:T(8,128)(2,1)} async-done(((bf16[64,8,3584]{2,1,0:T(8,128)(2,1)}), bf16[64,8,3584]{2,1,0:T(8,128)(2,1)}, u32[]{:S(2)}, u32[]{:S(2)}) %all-to-all-start) | async-done | bytes 3670048 | tf_op jit(solution)/shard_map/all_to_all | solution.py:112
  408.5 3.4 fusion.7
  413.1 3.0 fusion.2
  416.2 10.1 %all-to-all-start.2 = ((bf16[64,8,3584]{2,1,0:T(8,128)(2,1)}), bf16[64,8,3584]{2,1,0:T(8,128)(2,1)}, u32[]{:S(2)}, u32[]{:S(2)}) async-start(bf16[64,8,3584]{2,1,0:T(8,128)(2,1)} %fusion.2), calls=%async_computation.2 | async-start | bytes 7340032 | tf_op jit(solution)/shard_map/all_to_all | solution.py:151
  427.6 161.6 %all-to-all-done.2 = bf16[64,8,3584]{2,1,0:T(8,128)(2,1)} async-done(((bf16[64,8,3584]{2,1,0:T(8,128)(2,1)}), bf16[64,8,3584]{2,1,0:T(8,128)(2,1)}, u32[]{:S(2)}, u32[]{:S(2)}) %all-to-all-start.2) | async-done | bytes 3670048 | tf_op jit(solution)/shard_map/all_to_all | solution.py:151
  589.2 2.7 convolution_dynamic-update-slice_fusion.7
  591.9 2.8 convolution_dynamic-update-slice_fusion.6
  594.7 2.8 convolution_dynamic-update-slice_fusion.5
  597.5 2.9 convolution_dynamic-update-slice_fusion.4
  600.4 2.7 convolution_dynamic-update-slice_fusion.3
  603.1 2.7 convolution_dynamic-update-slice_fusion.2
  605.8 2.8 convolution_dynamic-update-slice_fusion.1
  608.7 2.8 convolution_dynamic-update-slice_fusion
  611.5 8.1 %reshape.114 = bf16[64,4,2,3584]{3,2,1,0:T(2,128)(2,1)} reshape(bf16[64,8,3584]{2,1,0:T(8,128)(2,1)} %all-to-all-done) | data formatting | bytes 7340032 | tf_op jit(solution)/shard_map/reshape | solution.py:142
  619.6 1.9 constant_dynamic-slice_fusion
  624.7 9.9 %all-to-all-start.3 = ((bf16[64,2,128]{2,1,0:T(2,128)(2,1)}), bf16[64,2,128]{2,1,0:T(2,128)(2,1)S(1)}, u32[]{:S(2)}, u32[]{:S(2)}) async-start(bf16[64,2,128]{2,1,0:T(2,128)(2,1)} %bitcast.22), calls=%async_computation.4 | async-start | bytes 65536 | tf_op jit(solution)/shard_map/all_to_all | solution.py:158
  634.8 12.4 %all-to-all-done.3 = bf16[64,2,128]{2,1,0:T(2,128)(2,1)S(1)} async-done(((bf16[64,2,128]{2,1,0:T(2,128)(2,1)}), bf16[64,2,128]{2,1,0:T(2,128)(2,1)S(1)}, u32[]{:S(2)}, u32[]{:S(2)}) %all-to-all-start.3) | async-done | bytes 32800 | tf_op jit(solution)/shard_map/all_to_all | solution.py:158
  648.0 2.8 reduce-scatter.2.cloned.1.call-done
  (55 shorter events, 11.0 us)
Async XLA Ops:
  7.2 616.4 %copy-start = (bf16[1,128,4096]{2,1,0:T(8,128)(2,1)S(1)}, bf16[1,128,4096]{2,1,0:T(8,128)(2,1)}, u32[]{:S(2)}) copy-start(bf16[1,128,4096]{2,1,0:T(8,128)(2,1)} %param.21) | copy-start | bytes 3145732
  7.2 45.0 %all-gather.8.cloned.1.call-start = ((), (), s32[]{:S(2)}) async-start(), calls=%async_computation.6 | async-start | bytes 2293760 | tf_op jit(solution)/shard_map/all_gather | solution.py:76
  56.6 16.4 %copy-start.6 = (bf16[64,1792]{1,0:T(8,128)(2,1)S(1)}, bf16[64,1792]{1,0:T(8,128)(2,1)}, u32[]{:S(2)}) copy-start(bf16[64,1792]{1,0:T(8,128)(2,1)} %param.12) | copy-start | bytes 688132
  56.6 179.1 %all-to-all-start.1 = ((bf16[64,8,3584]{2,1,0:T(8,128)(2,1)}), bf16[64,8,3584]{2,1,0:T(8,128)(2,1)}, u32[]{:S(2)}, u32[]{:S(2)}) async-start(bf16[64,8,3584]{2,1,0:T(8,128)(2,1)} %fusion.1), calls=%async_computation.1 | async-start | bytes 7340032 | tf_op jit(solution)/shard_map/all_to_all | solution.py:105
  72.9 39.5 %all-gather.6.cloned.1.call-start = ((), (), s32[]{:S(2)}) async-start(), calls=%async_computation.5 | async-start | bytes 2293760 | tf_op jit(solution)/shard_map/all_gather | solution.py:77
  116.9 128.8 %copy-start.1 = (bf16[1,3584,128]{2,1,0:T(8,128)(2,1)S(1)}, bf16[1,3584,128]{2,1,0:T(8,128)(2,1)}, u32[]{:S(2)}) copy-start(bf16[1,3584,128]{2,1,0:T(8,128)(2,1)} %param.16) | copy-start | bytes 2752516
  235.7 172.8 %all-to-all-start = ((bf16[64,8,3584]{2,1,0:T(8,128)(2,1)}), bf16[64,8,3584]{2,1,0:T(8,128)(2,1)}, u32[]{:S(2)}, u32[]{:S(2)}) async-start(bf16[64,8,3584]{2,1,0:T(8,128)(2,1)} %fusion), calls=%async_computation | async-start | bytes 7340032 | tf_op jit(solution)/shard_map/all_to_all | solution.py:112
  245.7 3.2 copy-start.2
  408.5 3.4 copy-start.3
  416.2 10.2 %copy-start.4 = (f32[512,128]{1,0:T(8,128)S(1)}, f32[512,128]{1,0:T(8,128)}, u32[]{:S(2)}) copy-start(f32[512,128]{1,0:T(8,128)} %fusion.5) | copy-start | bytes 786436
  416.2 10.2 %copy-start.9 = (bf16[1,64,128]{2,1,0:T(8,128)(2,1)S(1)}, bf16[1,64,128]{2,1,0:T(8,128)(2,1)}, u32[]{:S(2)}) copy-start(bf16[1,64,128]{2,1,0:T(8,128)(2,1)} %param.19) | copy-start | bytes 49156
  416.2 173.0 %all-to-all-start.2 = ((bf16[64,8,3584]{2,1,0:T(8,128)(2,1)}), bf16[64,8,3584]{2,1,0:T(8,128)(2,1)}, u32[]{:S(2)}, u32[]{:S(2)}) async-start(bf16[64,8,3584]{2,1,0:T(8,128)(2,1)} %fusion.2), calls=%async_computation.2 | async-start | bytes 7340032 | tf_op jit(solution)/shard_map/all_to_all | solution.py:151
  426.3 196.0 %all-reduce.2.cloned.1.call-start = ((), (), s32[]{:S(2)}) async-start(), calls=%async_computation.8 | async-start | bytes 524288 | tf_op jit(solution)/shard_map/psum | solution.py:136
  427.3 223.4 %reduce-scatter.2.cloned.1.call-start = ((), (), s32[]{:S(2)}) async-start(), calls=%async_computation.7 | async-start | bytes 4128768 | tf_op jit(solution)/shard_map/reduce_scatter | solution.py:174
  619.6 2.2 copy-start.5
  621.5 13.0 %copy-start.7 = (s32[64,8]{0,1:T(8,128)S(1)}, s32[64,8]{0,1:T(8,128)}, u32[]{:S(2)}) copy-start(s32[64,8]{0,1:T(8,128)} %param.14) | copy-start | bytes 6148
  621.5 13.0 %copy-start.8 = (s32[64,8]{0,1:T(8,128)S(1)}, s32[64,8]{0,1:T(8,128)}, u32[]{:S(2)}) copy-start(s32[64,8]{0,1:T(8,128)} %param.13) | copy-start | bytes 6148
  624.7 22.5 %all-to-all-start.3 = ((bf16[64,2,128]{2,1,0:T(2,128)(2,1)}), bf16[64,2,128]{2,1,0:T(2,128)(2,1)S(1)}, u32[]{:S(2)}, u32[]{:S(2)}) async-start(bf16[64,2,128]{2,1,0:T(2,128)(2,1)} %bitcast.22), calls=%async_computation.4 | async-start | bytes 65536 | tf_op jit(solution)/shard_map/all_to_all | solution.py:158
Sparse Core Ops, SparseCore 0:
  11.3 40.8 all-gather.7
  75.9 36.4 all-gather.5
  429.5 76.6 all-reduce.1
  611.6 39.0 reduce-scatter.1
where the time goes:
time: 660 us; the launch traced here: 659 us
  waiting for transfers between devices  491 us (74%)
  matrix products  49.1 us (7%)
  starting transfers between devices  46.7 us (7%)
  blocking collectives  41.8 us (6%)
  between operations  14.1 us (2%)
  local copies, waits for them, and re-layouts  12.1 us (2%)
    all_to_all x1, waiting for transfers between devices, on_device(): lax.all_to_all(parts.reshape(experts, rows_per, full_width), 'expert', sp...  162 us
    all_to_all x1, waiting for transfers between devices, on_device(): lax.all_to_all(grad_buf.reshape(experts, rows_per, full_width), 'expert',...  156 us
    all_to_all x1, waiting for transfers between devices, on_device(): lax.all_to_all(in_buf.reshape(experts, rows_per, full_width), 'expert', s...  119 us
    all_gather x1, waiting for transfers between devices, on_device(): lax.all_gather(full_grad, 'dp', axis=0, tiled=True)  37 us
    dot_general x8, matrix products, on_device(): lax.dot_general(picked_cols, part_cols, (((0,), (0,)), ((), ())), preferr...  22.3 us
    all_to_all x1, starting transfers between devices, on_device(): lax.all_to_all(in_buf.reshape(experts, rows_per, full_width), 'expert', s...  16.3 us
  transfers between devices with their start and end apart: 8, of which 7 were waited for; matrix products, arithmetic and copies ran while one was open for 8% of the time, Pallas kernels for 0%

commit v1 on v0

--- a/solution.py
+++ b/solution.py
@@ -74,7 +74,9 @@
     own_pick, own_weight = pick_tables(route_ids, route_slots, route_weight, experts)
     all_in, all_grad, all_ids, all_slots, all_weight = (
         lax.all_gather(full_in, "dp", axis=0, tiled=True),
-        lax.all_gather(full_grad, "dp", axis=0, tiled=True),
+        jnp.concatenate(
+            lax.all_to_all(jnp.stack([full_grad] * lax.axis_size("dp")), "dp", 0, 0), axis=0
+        ),
         lax.all_gather(route_ids, "dp", axis=0, tiled=True),
         lax.all_gather(route_slots, "dp", axis=0, tiled=True),
         lax.all_gather(route_weight, "dp", axis=0, tiled=True),

time: 660 us -> 667 us (1.011)
  the two profiles are of different devices: /device:TPU:4 before, /device:TPU:2 now
where the time goes in v1:
time: 667 us; the launch traced here: 666 us
  waiting for transfers between devices  473 us (71%)
  blocking collectives  56.1 us (8%)
  starting transfers between devices  54.4 us (8%)
  matrix products  47.8 us (7%)
  local copies, waits for them, and re-layouts  15.2 us (2%)
  between operations  14.1 us (2%)
    all_to_all x1, waiting for transfers between devices, on_device(): lax.all_to_all(parts.reshape(experts, rows_per, full_width), 'expert', sp...  158 us
    all_to_all x1, waiting for transfers between devices, on_device(): lax.all_to_all(in_buf.reshape(experts, rows_per, full_width), 'expert', s...  153 us
    all_to_all x1, waiting for transfers between devices, on_device(): lax.all_to_all(grad_buf.reshape(experts, rows_per, full_width), 'expert',...  111 us
    all_gather x1, waiting for transfers between devices, on_device(): lax.all_gather(full_in, 'dp', axis=0, tiled=True)  37 us
    all_gather x1, blocking collectives, on_device(): lax.all_gather(route_slots, 'dp', axis=0, tiled=True)  28.9 us
    dot_general x8, matrix products, on_device(): lax.dot_general(picked_cols, part_cols, (((0,), (0,)), ((), ())), preferr...  22.4 us
    all_to_all x1, starting transfers between devices, on_device(): lax.all_to_all(grad_buf.reshape(experts, rows_per, full_width), 'expert',...  18.9 us
  transfers between devices with their start and end apart: 8, of which 6 were waited for; matrix products, arithmetic and copies ran while one was open for 8% of the time, Pallas kernels for 0%

profile of v1, /device:TPU:2, one launch (start us, length us, event | category | flops | bytes accessed | tf_op | source)
XLA Modules:
  0.0 665.5 jit_solution(14494402430547614668)
XLA Ops:
  7.2 2.5 all_gather.21
  11.1 4.5 all-to-all-start
  15.6 28.9 %all-gather = s32[4,64,8]{1,2,0:T(8,128)S(1)} all-gather(s32[1,64,8]{1,2,0:T(8,128)S(1)} %bitcast.67), channel_id=1, replica_groups=mesh['expert'=64,'dp'=4,'test'=2] {'dp'}, dimensions={0}, use_global_device_ids=true | all-gather | bytes 10240 | tf_op jit(solution)/shard_map/all_gather | solution.py:81
  44.5 12.0 %all-gather.1 = s32[4,64,8]{1,2,0:T(8,128)S(1)} all-gather(s32[1,64,8]{1,2,0:T(8,128)S(1)} %bitcast.68), channel_id=1, replica_groups=mesh['expert'=64,'dp'=4,'test'=2] {'dp'}, dimensions={0}, use_global_device_ids=true | all-gather | bytes 10240 | tf_op jit(solution)/shard_map/all_gather | solution.py:80
  56.6 10.4 %all-gather.2 = bf16[4,64,8]{1,2,0:T(8,128)(2,1)S(1)} all-gather(bf16[1,64,8]{1,2,0:T(8,128)(2,1)S(1)} %bitcast.69), channel_id=1, replica_groups=mesh['expert'=64,'dp'=4,'test'=2] {'dp'}, dimensions={0}, use_global_device_ids=true | all-gather | bytes 5120 | tf_op jit(solution)/shard_map/all_gather | solution.py:82
  71.2 3.0 fusion
  74.2 18.9 %all-to-all-start.1 = ((bf16[64,8,3584]{2,1,0:T(8,128)(2,1)}), bf16[64,8,3584]{2,1,0:T(8,128)(2,1)}, u32[]{:S(2)}, u32[]{:S(2)}) async-start(bf16[64,8,3584]{2,1,0:T(8,128)(2,1)} %fusion), calls=%async_computation.1 | async-start | bytes 7340032 | tf_op jit(solution)/shard_map/all_to_all | solution.py:114
  93.2 2.3 all_gather.22
  95.6 37.0 %all-gather.5.cloned.1.call-done = bf16[256,3584]{1,0:T(8,128)(2,1)} async-done(((bf16[64,3584]{1,0:T(8,128)(2,1)}), bf16[256,3584]{1,0:T(8,128)(2,1)}) %all-gather.5.cloned.1.call-update) | async-done | bytes 1835024 | tf_op jit(solution)/shard_map/all_gather | solution.py:76
  132.6 4.5 fusion.1
  137.1 110.9 %all-to-all-done.1 = bf16[64,8,3584]{2,1,0:T(8,128)(2,1)} async-done(((bf16[64,8,3584]{2,1,0:T(8,128)(2,1)}), bf16[64,8,3584]{2,1,0:T(8,128)(2,1)}, u32[]{:S(2)}, u32[]{:S(2)}) %all-to-all-start.1) | async-done | bytes 3670048 | tf_op jit(solution)/shard_map/all_to_all | solution.py:114
  248.1 10.4 %all-to-all-start.2 = ((bf16[64,8,3584]{2,1,0:T(8,128)(2,1)}), bf16[64,8,3584]{2,1,0:T(8,128)(2,1)}, u32[]{:S(2)}, u32[]{:S(2)}) async-start(bf16[64,8,3584]{2,1,0:T(8,128)(2,1)} %fusion.1), calls=%async_computation.2 | async-start | bytes 7340032 | tf_op jit(solution)/shard_map/all_to_all | solution.py:107
  258.5 4.2 fusion.7
  262.7 152.5 %all-to-all-done.2 = bf16[64,8,3584]{2,1,0:T(8,128)(2,1)} async-done(((bf16[64,8,3584]{2,1,0:T(8,128)(2,1)}), bf16[64,8,3584]{2,1,0:T(8,128)(2,1)}, u32[]{:S(2)}, u32[]{:S(2)}) %all-to-all-start.2) | async-done | bytes 3670048 | tf_op jit(solution)/shard_map/all_to_all | solution.py:107
  415.2 3.2 fusion.3
  418.5 3.1 fusion.5
  423.4 3.1 fusion.2
  426.5 10.7 %all-to-all-start.3 = ((bf16[64,8,3584]{2,1,0:T(8,128)(2,1)}), bf16[64,8,3584]{2,1,0:T(8,128)(2,1)}, u32[]{:S(2)}, u32[]{:S(2)}) async-start(bf16[64,8,3584]{2,1,0:T(8,128)(2,1)} %fusion.2), calls=%async_computation.3 | async-start | bytes 7340032 | tf_op jit(solution)/shard_map/all_to_all | solution.py:153
  438.4 158.4 %all-to-all-done.3 = bf16[64,8,3584]{2,1,0:T(8,128)(2,1)} async-done(((bf16[64,8,3584]{2,1,0:T(8,128)(2,1)}), bf16[64,8,3584]{2,1,0:T(8,128)(2,1)}, u32[]{:S(2)}, u32[]{:S(2)}) %all-to-all-start.3) | async-done | bytes 3670048 | tf_op jit(solution)/shard_map/all_to_all | solution.py:153
  596.8 2.7 convolution_dynamic-update-slice_fusion.7
  599.5 2.8 convolution_dynamic-update-slice_fusion.6
  602.3 2.8 convolution_dynamic-update-slice_fusion.5
  605.2 2.9 convolution_dynamic-update-slice_fusion.4
  608.0 2.7 convolution_dynamic-update-slice_fusion.3
  610.8 2.7 convolution_dynamic-update-slice_fusion.2
  613.5 2.9 convolution_dynamic-update-slice_fusion.1
  616.3 2.8 convolution_dynamic-update-slice_fusion
  619.2 8.1 %reshape.128 = bf16[64,4,2,3584]{3,2,1,0:T(2,128)(2,1)} reshape(bf16[64,8,3584]{2,1,0:T(8,128)(2,1)} %all-to-all-done.1) | data formatting | bytes 7340032 | tf_op jit(solution)/shard_map/reshape | solution.py:144
  627.3 1.9 constant_dynamic-slice_fusion
  632.3 9.6 %all-to-all-start.4 = ((bf16[64,2,128]{2,1,0:T(2,128)(2,1)}), bf16[64,2,128]{2,1,0:T(2,128)(2,1)S(1)}, u32[]{:S(2)}, u32[]{:S(2)}) async-start(bf16[64,2,128]{2,1,0:T(2,128)(2,1)} %bitcast.23), calls=%async_computation.5 | async-start | bytes 65536 | tf_op jit(solution)/shard_map/all_to_all | solution.py:160
  642.2 13.2 %all-to-all-done.4 = bf16[64,2,128]{2,1,0:T(2,128)(2,1)S(1)} async-done(((bf16[64,2,128]{2,1,0:T(2,128)(2,1)}), bf16[64,2,128]{2,1,0:T(2,128)(2,1)S(1)}, u32[]{:S(2)}, u32[]{:S(2)}) %all-to-all-start.4) | async-done | bytes 32800 | tf_op jit(solution)/shard_map/all_to_all | solution.py:160
  657.2 1.7 convert_element_type.87
  (59 shorter events, 14.0 us)
Async XLA Ops:
  7.2 624.1 %copy-start = (bf16[1,128,4096]{2,1,0:T(8,128)(2,1)S(1)}, bf16[1,128,4096]{2,1,0:T(8,128)(2,1)}, u32[]{:S(2)}) copy-start(bf16[1,128,4096]{2,1,0:T(8,128)(2,1)} %param.21) | copy-start | bytes 3145732
  7.2 8.4 %copy-start.8 = (s32[64,8]{0,1:T(8,128)S(1)}, s32[64,8]{0,1:T(8,128)}, u32[]{:S(2)}) copy-start(s32[64,8]{0,1:T(8,128)} %param.14) | copy-start | bytes 6148
  7.2 37.3 %copy-start.9 = (s32[64,8]{0,1:T(8,128)S(1)}, s32[64,8]{0,1:T(8,128)}, u32[]{:S(2)}) copy-start(s32[64,8]{0,1:T(8,128)} %param.13) | copy-start | bytes 6148
  7.2 49.4 %copy-start.10 = (bf16[64,8]{0,1:T(8,128)(2,1)S(1)}, bf16[64,8]{0,1:T(8,128)(2,1)}, u32[]{:S(2)}) copy-start(bf16[64,8]{0,1:T(8,128)(2,1)} %param.15) | copy-start | bytes 3076
  11.1 60.1 %all-to-all-start = ((bf16[4,64,3584]{2,1,0:T(8,128)(2,1)}), bf16[4,64,3584]{2,1,0:T(8,128)(2,1)S(1)}, u32[]{:S(2)}, u32[]{:S(2)}) async-start(bf16[4,64,3584]{2,1,0:T(8,128)(2,1)} %stack.2), calls=%async_computation | async-start | bytes 3670016 | tf_op jit(solution)/shard_map/all_to_all | solution.py:78
  74.2 19.0 %copy-start.7 = (bf16[64,1792]{1,0:T(8,128)(2,1)S(1)}, bf16[64,1792]{1,0:T(8,128)(2,1)}, u32[]{:S(2)}) copy-start(bf16[64,1792]{1,0:T(8,128)(2,1)} %param.11) | copy-start | bytes 688132
  74.2 173.9 %all-to-all-start.1 = ((bf16[64,8,3584]{2,1,0:T(8,128)(2,1)}), bf16[64,8,3584]{2,1,0:T(8,128)(2,1)}, u32[]{:S(2)}, u32[]{:S(2)}) async-start(bf16[64,8,3584]{2,1,0:T(8,128)(2,1)} %fusion), calls=%async_computation.1 | async-start | bytes 7340032 | tf_op jit(solution)/shard_map/all_to_all | solution.py:114
  93.2 39.4 %all-gather.5.cloned.1.call-start = ((), (), s32[]{:S(2)}) async-start(), calls=%async_computation.6 | async-start | bytes 2293760 | tf_op jit(solution)/shard_map/all_gather | solution.py:76
  248.1 167.2 %all-to-all-start.2 = ((bf16[64,8,3584]{2,1,0:T(8,128)(2,1)}), bf16[64,8,3584]{2,1,0:T(8,128)(2,1)}, u32[]{:S(2)}, u32[]{:S(2)}) async-start(bf16[64,8,3584]{2,1,0:T(8,128)(2,1)} %fusion.1), calls=%async_computation.2 | async-start | bytes 7340032 | tf_op jit(solution)/shard_map/all_to_all | solution.py:107
  258.5 156.8 %copy-start.1 = (bf16[1,3584,128]{2,1,0:T(8,128)(2,1)S(1)}, bf16[1,3584,128]{2,1,0:T(8,128)(2,1)}, u32[]{:S(2)}) copy-start(bf16[1,3584,128]{2,1,0:T(8,128)(2,1)} %param.16) | copy-start | bytes 2752516
  258.5 160.0 %copy-start.2 = (bf16[1,3584,128]{2,1,0:T(8,128)(2,1)S(1)}, bf16[1,3584,128]{2,1,0:T(8,128)(2,1)}, u32[]{:S(2)}) copy-start(bf16[1,3584,128]{2,1,0:T(8,128)(2,1)} %param.17) | copy-start | bytes 2752516
  415.2 7.0 %copy-start.3 = (f32[512,128]{1,0:T(8,128)S(1)}, f32[512,128]{1,0:T(8,128)}, u32[]{:S(2)}) copy-start(f32[512,128]{1,0:T(8,128)} %fusion.7) | copy-start | bytes 786436
  421.6 0.7 copy-start.4
  426.5 10.7 %copy-start.5 = (f32[512,128]{1,0:T(8,128)S(1)}, f32[512,128]{1,0:T(8,128)}, u32[]{:S(2)}) copy-start(f32[512,128]{1,0:T(8,128)} %copy-done.4) | copy-start | bytes 786436
  426.5 10.7 %copy-start.11 = (bf16[1,64,128]{2,1,0:T(8,128)(2,1)S(1)}, bf16[1,64,128]{2,1,0:T(8,128)(2,1)}, u32[]{:S(2)}) copy-start(bf16[1,64,128]{2,1,0:T(8,128)(2,1)} %param.19) | copy-start | bytes 49156
  426.5 170.3 %all-to-all-start.3 = ((bf16[64,8,3584]{2,1,0:T(8,128)(2,1)}), bf16[64,8,3584]{2,1,0:T(8,128)(2,1)}, u32[]{:S(2)}, u32[]{:S(2)}) async-start(bf16[64,8,3584]{2,1,0:T(8,128)(2,1)} %fusion.2), calls=%async_computation.3 | async-start | bytes 7340032 | tf_op jit(solution)/shard_map/all_to_all | solution.py:153
  437.2 192.8 %all-reduce.2.cloned.1.call-start = ((), (), s32[]{:S(2)}) async-start(), calls=%async_computation.8 | async-start | bytes 524288 | tf_op jit(solution)/shard_map/psum | solution.py:138
  438.2 219.1 %reduce-scatter.2.cloned.1.call-start = ((), (), s32[]{:S(2)}) async-start(), calls=%async_computation.7 | async-start | bytes 4128768 | tf_op jit(solution)/shard_map/reduce_scatter | solution.py:176
  627.3 2.2 copy-start.6
  632.3 23.1 %all-to-all-start.4 = ((bf16[64,2,128]{2,1,0:T(2,128)(2,1)}), bf16[64,2,128]{2,1,0:T(2,128)(2,1)S(1)}, u32[]{:S(2)}, u32[]{:S(2)}) async-start(bf16[64,2,128]{2,1,0:T(2,128)(2,1)} %bitcast.23), calls=%async_computation.5 | async-start | bytes 65536 | tf_op jit(solution)/shard_map/all_to_all | solution.py:160
Sparse Core Ops, SparseCore 0:
  96.1 36.4 all-gather.4
  440.3 76.4 all-reduce.1
  619.3 37.8 reduce-scatter.1
